TPU v7x, 32 devices: a whole 2x2x4 slice. The times are simulated.
32 devices in a mesh: side: 4 (over y, x), edge: 8 (over z, core).
Axes of the slice: x: 2, y: 2, z: 4, core: 2. Of those that a mesh axis runs over, the one named last changes fastest.
Arguments:
- parent_blocks: bfloat16 [32, 450, 128], P(('side', 'edge')), may hold values from -6 to 6
- interp_weight: bfloat16 [128, 2, 128, 128], P(('side', 'edge')), may hold values from -0.375 to 0.375
- tile_source: int32 [128, 2], P(('side', 'edge')), may hold values from 0 to 31, as said below
- destination: int32 [16384, 1], P(('side', 'edge')), may hold values from 0 to 7; in each aligned block of 512 rows (0 to 511, 512 to 1023, ...) at most 128 rows name the same one
- remap_matrix: bfloat16 [5, 400, 90], replicated, may hold values from -0.625 to 0.625
Outputs:
- forcing: bfloat16 [5, 400, 32768], P(None, None, ('side', 'edge'))
Inputs may be any that keep to these rules, and one draw needn't show every extreme that they name: `tile_source`: the two blocks of a tile are distinct, and each is the tile's own device d or d - 1 or d + 1 modulo 32 along the loop of devices. `destination`: among the rows of one device no owner is named more than 128 times, and in some devices some owner is named exactly 128 times.
All inputs are finite; a program needn't handle non-finite values.
Results may differ from a plain program's by a relative error of at most 0.0049.
Values may be sent and summed in bfloat16 or wider, within the bound.
No kernel may reach another device: no remote copies, remote signals or barrier semaphores. Data moves between devices by JAX's collectives and lax.ppermute only.
A program may use at most 64 MiB of HBM per device.

v0:
```python
import jax
import jax.numpy as jnp
from jax import lax
from jax.sharding import PartitionSpec as P


def padded(array, sides, width):
    for axis, dim in sides:
        devices, length = (lax.axis_size(axis), array.shape[dim])
        up = [(i, (i + 1) % devices) for i in range(devices)]
        down = [(j, i) for i, j in up]
        last = lax.slice_in_dim(array, length - width, length, axis=dim)
        leading = lax.slice_in_dim(array, 0, width, axis=dim)
        before = lax.ppermute(last, axis, up)
        after = lax.ppermute(leading, axis, down)
        array = jnp.concatenate([before, array, after], axis=dim)
    return array


def remap_rows(remap_matrix, rows):
    shaped = rows.reshape(remap_matrix.shape[0], remap_matrix.shape[2], rows.shape[1])
    result = jnp.einsum("vcl,vln->vcn", remap_matrix, shaped, preferred_element_type=jnp.float32)
    return result.astype(jnp.bfloat16)


def body(parent_blocks, interp_weight, tile_source, destination, remap_matrix):
    edge_count = lax.axis_size("edge")
    block_count = lax.axis_size("side") * edge_count
    position = lax.axis_index("side") * edge_count + lax.axis_index("edge")
    rim_blocks = padded(parent_blocks, ((("side", "edge"), 0),), 1)
    offset = (tile_source - position + 1 + block_count) % block_count
    chosen = rim_blocks[offset]
    summed = jnp.einsum("tkfp,tkpr->tfr", chosen, interp_weight, preferred_element_type=jnp.float32)
    coarse = summed.astype(jnp.bfloat16)
    tile_count, feat_count, tile_rows = coarse.shape
    rows = coarse.transpose(1, 0, 2).reshape(feat_count, tile_count * tile_rows)
    row_count = destination.shape[0]
    capacity = max(2, 2 * row_count // edge_count)
    owners = destination[:, 0]
    owner_hits = (owners[:, None] == jnp.arange(edge_count, dtype=jnp.int32)[None, :]).astype(
        jnp.int32
    )
    places = jnp.sum(jnp.cumsum(owner_hits, axis=0) * owner_hits, axis=1) - 1
    slot_index = owners * capacity + places
    outbox = (
        jnp.zeros((feat_count, edge_count * capacity), jnp.bfloat16).at[:, slot_index].set(rows)
    )
    inbox = lax.all_to_all(outbox, "edge", split_axis=1, concat_axis=1, tiled=True)
    forcing = remap_rows(remap_matrix, inbox)
    return forcing


def solution(mesh):
    return jax.shard_map(
        body,
        mesh=mesh,
        in_specs=(
            P(("side", "edge"), None, None),
            P(("side", "edge"), None, None, None),
            P(("side", "edge"), None),
            P(("side", "edge"), None),
            P(),
        ),
        out_specs=P(None, None, ("side", "edge")),
        check_vma=False,
    )
```

profile of v0, /device:TPU:0, one launch (start us, length us, event | category | flops | bytes accessed | tf_op | source)
XLA Modules:
  0.0 49.2 jit_solution(1207886696506333563)
XLA Ops:
  0.0 0.0 copy-start
  0.0 0.5 collective-permute-start
  0.5 6.0 %collective-permute-start.1 = (bf16[1,450,128]{2,1,0:T(8,128)(2,1)}, bf16[1,450,128]{2,1,0:T(8,128)(2,1)S(1)}, u32[]{:S(2)}, u32[]{:S(2)}) collective-permute-start(bf16[1,450,128]{2,1,0:T(8,128)(2,1)} %param.5), channel_id=1, source_target_pairs={{1,0},{2,1},{3,2},{4,3},{5,4},{6,5},{7,6},{8,7},{9,8},{10,9},{11,1... | collective-permute-start | bytes 345608 | tf_op jit(solution)/shard_map/ppermute | solution.py:15
  6.4 0.7 %fusion.5 = s32[8,4,128]{2,0,1:T(8,128)S(1)} fusion(s32[4,128]{1,0:T(4,128)} %bitcast.37), kind=kLoop, calls=%fused_computation.14 | loop fusion | flops 8192 | bytes 18432 | tf_op jit(solution)/shard_map/convert_element_type | solution.py:40
  7.1 1.1 %reduce-window.6 = s32[8,4,128]{2,0,1:T(8,128)S(1)} reduce-window(s32[8,4,128]{2,0,1:T(8,128)S(1)} %fusion.5, s32[]{:T(128)} %constant.21.clone.1), window={size=1x1x128 pad=0_0x0_0x127_0}, to_apply=%region_0.1 | reduce-window | flops 520192 | bytes 32772 | tf_op jit(solution)/shard_map/reduce-window
  8.2 0.2 slice_reduce_fusion
  8.5 0.8 %fusion.4 = s32[512]{0:T(512)S(1)} fusion(s32[8,4,128]{2,0,1:T(8,128)S(1)} %reduce-window.6, s32[8,4]{0,1:T(4,128)S(1)} %slice.7, s32[512]{0:T(512)} %bitcast.38), kind=kLoop, calls=%fused_computation.11 | loop fusion | flops 15872 | bytes 20608 | tf_op jit(solution)/shard_map/reduce_sum | solution.py:43
  9.3 0.7 %compare_select_fusion = s32[512,1]{0,1:T(1,128)S(1)} fusion(s32[512,1]{0,1:T(1,128)S(1)} %bitcast.39, s32[512,1]{0,1:T(1,128)} %param.8), kind=kLoop, calls=%fused_computation.15 | loop fusion | flops 2560 | bytes 6144 | tf_op jit(solution)/shard_map/select_n | solution.py:46
  10.0 0.7 %compare_select_fusion.1 = s32[4,2]{0,1:T(2,128)S(1)} fusion(s32[4,2]{0,1:T(2,128)} %param.7, s32[]{:T(128)S(6)} %add.43), kind=kLoop, calls=%fused_computation.17 | loop fusion | flops 128 | bytes 68 | tf_op jit(solution)/shard_map/select_n | solution.py:32
  10.7 0.1 copy.12
  10.8 0.1 reshape.39
  10.9 0.0 collective-permute-done
  10.9 0.0 collective-permute-done.1
  10.9 0.9 %pad_maximum_fusion = bf16[3,450,128]{2,1,0:T(8,128)(2,1)S(1)} fusion(bf16[1,450,128]{2,1,0:T(8,128)(2,1)S(1)} %collective-permute-done.1, bf16[1,450,128]{2,1,0:T(8,128)(2,1)} %param.5, bf16[1,450,128]{2,1,0:T(8,128)(2,1)S(1)} %collective-permute-done), kind=kLoop, calls=%fused_computation.8 | loop fusion | flops 345600 | bytes 691200 | tf_op jit(solution)/shard_map/concatenate | solution.py:16
  11.8 0.7 %gather_fusion = bf16[8,450,128]{2,1,0:T(8,128)(2,1)S(1)} fusion(bf16[3,450,128]{2,1,0:T(8,128)(2,1)S(1)} %pad_maximum_fusion, s32[1024]{0:T(1024)S(1)} %pad_clamp_fusion), kind=kCustom, calls=%fused_computation | custom fusion | bytes 1843232 | tf_op jit(solution)/shard_map/gather | solution.py:32
  12.5 1.4 %fusion.1 = bf16[450,4,128]{2,0,1:T(8,128)(2,1)S(1)} fusion(bf16[4,2,450,128]{3,2,1,0:T(8,128)(2,1)S(1)} %bitcast.34, bf16[4,2,128,128]{3,2,1,0:T(8,128)(2,1)} %param.6), kind=kOutput, calls=%fused_computation.5 | convolution fusion | flops 118195200 | bytes 1644544 | tf_op jit(solution)/shard_map/tkfp,tkpr->tfr/dot_general | solution.py:33
  13.9 0.2 copy.13
  14.1 0.2 pad.4
  14.3 0.1 copy.18
  14.4 0.2 copy.14
  14.6 2.7 %scatter_custom_fusion = bf16[450,1024]{0,1:T(8,128)(2,1)S(1)} fusion(s32[512]{0:T(512)S(1)} %bitcast.40, bf16[512,450]{1,0:T(8,128)(2,1)S(1)} %copy.14, bf16[]{:T(256)} %constant.16.clone.1), kind=kCustom, calls=%fused_computation.6 | custom fusion | bytes 921602 | tf_op jit(solution)/shard_map/scatter | solution.py:46
  17.3 0.6 %copy.15 = bf16[450,8,128]{2,0,1:T(8,128)(2,1)S(1)} copy(bf16[450,8,128]{0,2,1:T(8,128)(2,1)S(1)} %bitcast.33) | data formatting | bytes 1843200 | tf_op jit(solution)/shard_map/all_to_all | solution.py:48
  18.0 27.4 %all_to_all.9 = bf16[450,8,128]{2,0,1:T(8,128)(2,1)S(1)} all-to-all(bf16[450,8,128]{2,0,1:T(8,128)(2,1)S(1)} %copy.15), channel_id=1, replica_groups=mesh['side'=4,'edge'=8] {'edge'}, dimensions={1} | all-to-all | bytes 1843200 | tf_op jit(solution)/shard_map/all_to_all | solution.py:48
  45.4 0.1 copy.16
  45.5 0.4 reshape.36
  45.9 0.0 copy-done
  45.9 3.2 %convert_bitcast_fusion = bf16[5,400,1024]{2,1,0:T(8,128)(2,1)} fusion(bf16[5,90,1024]{2,1,0:T(8,128)(2,1)S(1)} %reshape.36, bf16[5,400,90]{1,2,0:T(8,128)(2,1)S(1)} %copy-done), kind=kOutput, calls=%fused_computation.2 | convolution fusion | flops 370688000 | bytes 5377600 | tf_op jit(solution)/shard_map/vcl,vln->vcn/dot_general | solution.py:22
  (4 shorter events, 0.1 us)
Async XLA Ops:
  0.0 45.9 %copy-start = (bf16[5,400,90]{1,2,0:T(8,128)(2,1)S(1)}, bf16[5,400,90]{1,2,0:T(8,128)(2,1)}, u32[]{:S(2)}) copy-start(bf16[5,400,90]{1,2,0:T(8,128)(2,1)} %param.9) | copy-start | bytes 1080004
  0.0 10.9 %collective-permute-start = (bf16[1,450,128]{2,1,0:T(8,128)(2,1)}, bf16[1,450,128]{2,1,0:T(8,128)(2,1)S(1)}, u32[]{:S(2)}, u32[]{:S(2)}) collective-permute-start(bf16[1,450,128]{2,1,0:T(8,128)(2,1)} %param.5), channel_id=1, source_target_pairs={{0,1},{1,2},{2,3},{3,4},{4,5},{5,6},{6,7},{7,8},{8,9},{9,10},{10,1... | collective-permute-start | bytes 345608 | tf_op jit(solution)/shard_map/ppermute | solution.py:14
  0.5 10.4 %collective-permute-start.1 = (bf16[1,450,128]{2,1,0:T(8,128)(2,1)}, bf16[1,450,128]{2,1,0:T(8,128)(2,1)S(1)}, u32[]{:S(2)}, u32[]{:S(2)}) collective-permute-start(bf16[1,450,128]{2,1,0:T(8,128)(2,1)} %param.5), channel_id=1, source_target_pairs={{1,0},{2,1},{3,2},{4,3},{5,4},{6,5},{7,6},{8,7},{9,8},{10,9},{11,1... | collective-permute-start | bytes 345608 | tf_op jit(solution)/shard_map/ppermute | solution.py:15
where the time goes:
time: 49.4 us; the launch traced here: 49.2 us
  blocking collectives  27.4 us (55%)
  starting transfers between devices  6.43 us (13%)
  local copies, waits for them, and re-layouts  5.66 us (11%)
  other arithmetic  4.95 us (10%)
  matrix products  4.61 us (9%)
    all_to_all x1, blocking collectives, body(): lax.all_to_all(outbox, 'edge', split_axis=1, concat_axis=1, tiled=True)  27.4 us
    ppermute x1, starting transfers between devices, padded(): after = lax.ppermute(leading, axis, down)  5.98 us
    dot_general x1, matrix products, remap_rows(): jnp.einsum('vcl,vln->vcn', remap_matrix, shaped, preferred_element_type=j...  3.24 us
    scatter x1, local copies, waits for them, and re-layouts, body(): jnp.zeros((feat_count, edge_count * capacity), jnp.bfloat16)  2.74 us
    dot_general x1, matrix products, body(): jnp.einsum('tkfp,tkpr->tfr', chosen, interp_weight, preferred_element_typ...  1.36 us
    another operation x2, other arithmetic  1.16 us
  transfers between devices with their start and end apart: 2, of which 0 were waited for; matrix products, arithmetic and copies ran while one was open for 9% of the time, Pallas kernels for 0%

commit v1 on v0

--- a/solution.py
+++ b/solution.py
@@ -2,6 +2,28 @@
 import jax.numpy as jnp
 from jax import lax
 from jax.sharding import PartitionSpec as P
+
+
+def in_blocks(x, dim, size):
+    before, after = (x.shape[:dim], x.shape[dim + 1 :])
+    return jnp.moveaxis(x.reshape(*before, size, -1, *after), dim, 0)
+
+
+def in_order(tiles, dim):
+    tiles = jnp.moveaxis(tiles, 0, dim)
+    dims = tiles.shape
+    return tiles.reshape(*dims[:dim], dims[dim] * dims[dim + 1], *dims[dim + 2 :])
+
+
+def exchange_in_pairs(x, axis, split_dim, concat_dim):
+    size, place = (lax.axis_size(axis), lax.axis_index(axis))
+    pieces = in_blocks(x, split_dim, size)
+    outs = [pieces[place]]
+    for step in range(1, size):
+        sent = pieces[place ^ step]
+        outs.append(lax.ppermute(sent, axis, [(i, i ^ step) for i in range(size)]))
+    pieces = jnp.stack(outs)[place ^ jnp.arange(size)]
+    return in_order(pieces, concat_dim)
 
 
 def padded(array, sides, width):
@@ -45,7 +67,7 @@
     outbox = (
         jnp.zeros((feat_count, edge_count * capacity), jnp.bfloat16).at[:, slot_index].set(rows)
     )
-    inbox = lax.all_to_all(outbox, "edge", split_axis=1, concat_axis=1, tiled=True)
+    inbox = exchange_in_pairs(outbox, "edge", 1, 1)
     forcing = remap_rows(remap_matrix, inbox)
     return forcing
 

time: 49.4 us -> 47.7 us (0.966)
  the two profiles are of different devices: /device:TPU:0 before, /device:TPU:19 now
where the time goes in v1:
time: 47.7 us; the launch traced here: 47.4 us
  waiting for transfers between devices  19.2 us (40%)
  starting transfers between devices  11.3 us (24%)
  local copies, waits for them, and re-layouts  7.15 us (15%)
  other arithmetic  4.96 us (10%)
  matrix products  4.61 us (10%)
    ppermute x7, waiting for transfers between devices, exchange_in_pairs(): outs.append(lax.ppermute(sent, axis, [(i, i ^ step) for i in range(size)]))  19.2 us
    ppermute x7, starting transfers between devices, exchange_in_pairs(): outs.append(lax.ppermute(sent, axis, [(i, i ^ step) for i in range(size)]))  9.4 us
    dot_general x1, matrix products, remap_rows(): jnp.einsum('vcl,vln->vcn', remap_matrix, shaped, preferred_element_type=j...  3.24 us
    scatter x1, local copies, waits for them, and re-layouts, body(): jnp.zeros((feat_count, edge_count * capacity), jnp.bfloat16)  2.74 us
    ppermute x1, starting transfers between devices, padded(): before = lax.ppermute(last, axis, up)  1.86 us
    dot_general x1, matrix products, body(): jnp.einsum('tkfp,tkpr->tfr', chosen, interp_weight, preferred_element_typ...  1.36 us
    another operation x10, local copies, waits for them, and re-layouts  1.26 us
    another operation x2, other arithmetic  1.16 us
  transfers between devices with their start and end apart: 9, of which 5 were waited for; matrix products, arithmetic and copies ran while one was open for 10% of the time, Pallas kernels for 0%

profile of v1, /device:TPU:19, one launch (start us, length us, event | category | flops | bytes accessed | tf_op | source)
XLA Modules:
  0.0 47.4 jit_solution(12308929285116317781)
XLA Ops:
  0.0 0.0 copy-start
  0.0 1.9 %collective-permute-start = (bf16[1,450,128]{2,1,0:T(8,128)(2,1)}, bf16[1,450,128]{2,1,0:T(8,128)(2,1)S(1)}, u32[]{:S(2)}, u32[]{:S(2)}) collective-permute-start(bf16[1,450,128]{2,1,0:T(8,128)(2,1)} %param.5), channel_id=1, source_target_pairs={{0,1},{1,2},{2,3},{3,4},{4,5},{5,6},{6,7},{7,8},{8,9},{9,10},{10,1... | collective-permute-start | bytes 345608 | tf_op jit(solution)/shard_map/ppermute | solution.py:36
  1.9 0.0 collective-permute-start.1
  1.9 0.7 %compare_select_fusion.1 = s32[4,2]{0,1:T(2,128)S(1)} fusion(s32[4,2]{0,1:T(2,128)} %param.7, s32[]{:T(128)S(6)} %add.77), kind=kLoop, calls=%fused_computation.27 | loop fusion | flops 128 | bytes 68 | tf_op jit(solution)/shard_map/select_n | solution.py:54
  2.6 0.1 copy.18
  2.7 0.1 reshape.67
  2.7 0.7 %fusion.5 = s32[8,4,128]{2,0,1:T(8,128)S(1)} fusion(s32[4,128]{1,0:T(4,128)} %bitcast.71), kind=kLoop, calls=%fused_computation.23 | loop fusion | flops 8192 | bytes 18432 | tf_op jit(solution)/shard_map/convert_element_type | solution.py:62
  3.4 1.1 %reduce-window.6 = s32[8,4,128]{2,0,1:T(8,128)S(1)} reduce-window(s32[8,4,128]{2,0,1:T(8,128)S(1)} %fusion.5, s32[]{:T(128)} %constant.20.clone.1), window={size=1x1x128 pad=0_0x0_0x127_0}, to_apply=%region_0.1 | reduce-window | flops 520192 | bytes 32772 | tf_op jit(solution)/shard_map/reduce-window
  4.6 0.2 slice_reduce_fusion
  4.8 0.8 %fusion.4 = s32[512]{0:T(512)S(1)} fusion(s32[8,4,128]{2,0,1:T(8,128)S(1)} %reduce-window.6, s32[8,4]{0,1:T(4,128)S(1)} %slice.7, s32[512]{0:T(512)} %bitcast.72), kind=kLoop, calls=%fused_computation.20 | loop fusion | flops 15872 | bytes 20608 | tf_op jit(solution)/shard_map/reduce_sum | solution.py:65
  5.6 0.7 %compare_select_fusion = s32[512,1]{0,1:T(1,128)S(1)} fusion(s32[512,1]{0,1:T(1,128)S(1)} %bitcast.73, s32[512,1]{0,1:T(1,128)} %param.8), kind=kLoop, calls=%fused_computation.24 | loop fusion | flops 2560 | bytes 6144 | tf_op jit(solution)/shard_map/select_n | solution.py:68
  6.3 0.0 collective-permute-done
  6.4 0.0 collective-permute-done.1
  6.4 0.9 %pad_maximum_fusion = bf16[3,450,128]{2,1,0:T(8,128)(2,1)S(1)} fusion(bf16[1,450,128]{2,1,0:T(8,128)(2,1)S(1)} %collective-permute-done.1, bf16[1,450,128]{2,1,0:T(8,128)(2,1)} %param.5, bf16[1,450,128]{2,1,0:T(8,128)(2,1)S(1)} %collective-permute-done), kind=kLoop, calls=%fused_computation.9 | loop fusion | flops 345600 | bytes 691200 | tf_op jit(solution)/shard_map/concatenate | solution.py:38
  7.3 0.7 %gather_fusion = bf16[8,450,128]{2,1,0:T(8,128)(2,1)S(1)} fusion(bf16[3,450,128]{2,1,0:T(8,128)(2,1)S(1)} %pad_maximum_fusion, s32[1024]{0:T(1024)S(1)} %pad_clamp_fusion.1), kind=kCustom, calls=%fused_computation | custom fusion | bytes 1843232 | tf_op jit(solution)/shard_map/gather | solution.py:54
  8.1 1.4 %fusion.1 = bf16[450,4,128]{2,0,1:T(8,128)(2,1)S(1)} fusion(bf16[4,2,450,128]{3,2,1,0:T(8,128)(2,1)S(1)} %bitcast.60, bf16[4,2,128,128]{3,2,1,0:T(8,128)(2,1)} %param.6), kind=kOutput, calls=%fused_computation.6 | convolution fusion | flops 118195200 | bytes 1644544 | tf_op jit(solution)/shard_map/tkfp,tkpr->tfr/dot_general | solution.py:55
  9.4 0.2 copy.19
  9.6 0.2 pad.5
  9.8 0.1 copy.31
  9.9 0.2 copy.20
  10.1 2.7 %scatter_custom_fusion = bf16[450,1024]{0,1:T(8,128)(2,1)S(1)} fusion(s32[512]{0:T(512)S(1)} %bitcast.74, bf16[512,450]{1,0:T(8,128)(2,1)S(1)} %copy.20, bf16[]{:T(256)} %constant.18.clone.1), kind=kCustom, calls=%fused_computation.7 | custom fusion | bytes 921602 | tf_op jit(solution)/shard_map/scatter | solution.py:68
  12.8 0.1 constant_dynamic-slice_fusion
  12.9 0.1 copy.28
  13.1 0.1 copy.27
  13.2 0.1 copy.26
  13.4 0.1 copy.25
  13.5 0.1 copy.24
  13.7 0.1 copy.23
  13.8 0.1 copy.22
  14.0 0.1 copy.21
  14.1 0.6 %collective-permute-start.2 = (bf16[450,128]{1,0:T(8,128)(2,1)S(1)}, bf16[450,128]{1,0:T(8,128)(2,1)S(1)}, u32[]{:S(2)}, u32[]{:S(2)}) collective-permute-start(bf16[450,128]{1,0:T(8,128)(2,1)S(1)} %bitcast.70), channel_id=1, source_target_pairs={{0,1},{1,0},{2,3},{3,2},{4,5},{5,4},{6,7},{7,6},{8,9},{9,8},{10,11... | collective-permute-start | bytes 345608 | tf_op jit(solution)/shard_map/ppermute | solution.py:24
  14.7 3.9 %collective-permute-start.3 = (bf16[450,128]{1,0:T(8,128)(2,1)S(1)}, bf16[450,128]{1,0:T(8,128)(2,1)S(1)}, u32[]{:S(2)}, u32[]{:S(2)}) collective-permute-start(bf16[450,128]{1,0:T(8,128)(2,1)S(1)} %bitcast.69), channel_id=1, source_target_pairs={{0,2},{1,3},{2,0},{3,1},{4,6},{5,7},{6,4},{7,5},{8,10},{9,11},{10,... | collective-permute-start | bytes 345608 | tf_op jit(solution)/shard_map/ppermute | solution.py:24
  18.6 0.3 collective-permute-start.4
  19.0 0.2 collective-permute-start.5
  19.2 2.7 %collective-permute-start.6 = (bf16[450,128]{1,0:T(8,128)(2,1)S(1)}, bf16[450,128]{1,0:T(8,128)(2,1)S(1)}, u32[]{:S(2)}, u32[]{:S(2)}) collective-permute-start(bf16[450,128]{1,0:T(8,128)(2,1)S(1)} %bitcast.66), channel_id=1, source_target_pairs={{0,5},{1,4},{2,7},{3,6},{4,1},{5,0},{6,3},{7,2},{8,13},{9,12},{10,... | collective-permute-start | bytes 345608 | tf_op jit(solution)/shard_map/ppermute | solution.py:24
  21.9 0.0 collective-permute-done.2
  21.9 0.1 collective-permute-start.7
  22.0 0.0 collective-permute-done.3
  22.0 1.6 %collective-permute-start.8 = (bf16[450,128]{1,0:T(8,128)(2,1)S(1)}, bf16[450,128]{1,0:T(8,128)(2,1)S(1)}, u32[]{:S(2)}, u32[]{:S(2)}) collective-permute-start(bf16[450,128]{1,0:T(8,128)(2,1)S(1)} %bitcast.64), channel_id=1, source_target_pairs={{0,7},{1,6},{2,5},{3,4},{4,3},{5,2},{6,1},{7,0},{8,15},{9,14},{10,... | collective-permute-start | bytes 345608 | tf_op jit(solution)/shard_map/ppermute | solution.py:24
  23.6 1.7 %collective-permute-done.4 = bf16[450,128]{1,0:T(8,128)(2,1)S(1)} collective-permute-done((bf16[450,128]{1,0:T(8,128)(2,1)S(1)}, bf16[450,128]{1,0:T(8,128)(2,1)S(1)}, u32[]{:S(2)}, u32[]{:S(2)}) %collective-permute-start.4) | collective-permute-done | bytes 115232 | tf_op jit(solution)/shard_map/ppermute | solution.py:24
  25.3 0.7 %collective-permute-done.5 = bf16[450,128]{1,0:T(8,128)(2,1)S(1)} collective-permute-done((bf16[450,128]{1,0:T(8,128)(2,1)S(1)}, bf16[450,128]{1,0:T(8,128)(2,1)S(1)}, u32[]{:S(2)}, u32[]{:S(2)}) %collective-permute-start.5) | collective-permute-done | bytes 115232 | tf_op jit(solution)/shard_map/ppermute | solution.py:24
  26.0 8.8 %collective-permute-done.6 = bf16[450,128]{1,0:T(8,128)(2,1)S(1)} collective-permute-done((bf16[450,128]{1,0:T(8,128)(2,1)S(1)}, bf16[450,128]{1,0:T(8,128)(2,1)S(1)}, u32[]{:S(2)}, u32[]{:S(2)}) %collective-permute-start.6) | collective-permute-done | bytes 115232 | tf_op jit(solution)/shard_map/ppermute | solution.py:24
  34.9 5.5 %collective-permute-done.7 = bf16[450,128]{1,0:T(8,128)(2,1)S(1)} collective-permute-done((bf16[450,128]{1,0:T(8,128)(2,1)S(1)}, bf16[450,128]{1,0:T(8,128)(2,1)S(1)}, u32[]{:S(2)}, u32[]{:S(2)}) %collective-permute-start.7) | collective-permute-done | bytes 115232 | tf_op jit(solution)/shard_map/ppermute | solution.py:24
  40.4 2.5 %collective-permute-done.8 = bf16[450,128]{1,0:T(8,128)(2,1)S(1)} collective-permute-done((bf16[450,128]{1,0:T(8,128)(2,1)S(1)}, bf16[450,128]{1,0:T(8,128)(2,1)S(1)}, u32[]{:S(2)}, u32[]{:S(2)}) %collective-permute-start.8) | collective-permute-done | bytes 115232 | tf_op jit(solution)/shard_map/ppermute | solution.py:24
  42.9 0.7 %gather_fusion.1 = bf16[8,450,128]{2,1,0:T(8,128)(2,1)S(1)} fusion(bf16[8,450,128]{2,1,0:T(8,128)(2,1)S(1)} %bitcast_dynamic-update-slice_fusion, s32[1024]{0:T(1024)S(1)} %pad_clamp_fusion), kind=kCustom, calls=%fused_computation.1 | custom fusion | bytes 1843232 | tf_op jit(solution)/shard_map/gather | solution.py:25
  43.6 0.1 copy.29
  43.8 0.4 reshape_reshape.3
  44.2 3.2 %convert_bitcast_fusion = bf16[5,400,1024]{2,1,0:T(8,128)(2,1)} fusion(bf16[5,90,1024]{2,1,0:T(8,128)(2,1)S(1)} %reshape_reshape.3, bf16[5,400,90]{1,2,0:T(8,128)(2,1)S(1)} %copy-done), kind=kOutput, calls=%fused_computation.3 | convolution fusion | flops 370688000 | bytes 5377600 | tf_op jit(solution)/shard_map/vcl,vln->vcn/dot_general | solution.py:44
  (15 shorter events, 0.2 us)
Async XLA Ops:
  0.0 44.2 %copy-start = (bf16[5,400,90]{1,2,0:T(8,128)(2,1)S(1)}, bf16[5,400,90]{1,2,0:T(8,128)(2,1)}, u32[]{:S(2)}) copy-start(bf16[5,400,90]{1,2,0:T(8,128)(2,1)} %param.9) | copy-start | bytes 1080004
  0.0 6.3 %collective-permute-start = (bf16[1,450,128]{2,1,0:T(8,128)(2,1)}, bf16[1,450,128]{2,1,0:T(8,128)(2,1)S(1)}, u32[]{:S(2)}, u32[]{:S(2)}) collective-permute-start(bf16[1,450,128]{2,1,0:T(8,128)(2,1)} %param.5), channel_id=1, source_target_pairs={{0,1},{1,2},{2,3},{3,4},{4,5},{5,6},{6,7},{7,8},{8,9},{9,10},{10,1... | collective-permute-start | bytes 345608 | tf_op jit(solution)/shard_map/ppermute | solution.py:36
  1.9 4.5 %collective-permute-start.1 = (bf16[1,450,128]{2,1,0:T(8,128)(2,1)}, bf16[1,450,128]{2,1,0:T(8,128)(2,1)S(1)}, u32[]{:S(2)}, u32[]{:S(2)}) collective-permute-start(bf16[1,450,128]{2,1,0:T(8,128)(2,1)} %param.5), channel_id=1, source_target_pairs={{1,0},{2,1},{3,2},{4,3},{5,4},{6,5},{7,6},{8,7},{9,8},{10,9},{11,1... | collective-permute-start | bytes 345608 | tf_op jit(solution)/shard_map/ppermute | solution.py:37
  14.1 7.8 %collective-permute-start.2 = (bf16[450,128]{1,0:T(8,128)(2,1)S(1)}, bf16[450,128]{1,0:T(8,128)(2,1)S(1)}, u32[]{:S(2)}, u32[]{:S(2)}) collective-permute-start(bf16[450,128]{1,0:T(8,128)(2,1)S(1)} %bitcast.70), channel_id=1, source_target_pairs={{0,1},{1,0},{2,3},{3,2},{4,5},{5,4},{6,7},{7,6},{8,9},{9,8},{10,11... | collective-permute-start | bytes 345608 | tf_op jit(solution)/shard_map/ppermute | solution.py:24
  14.7 7.3 %collective-permute-start.3 = (bf16[450,128]{1,0:T(8,128)(2,1)S(1)}, bf16[450,128]{1,0:T(8,128)(2,1)S(1)}, u32[]{:S(2)}, u32[]{:S(2)}) collective-permute-start(bf16[450,128]{1,0:T(8,128)(2,1)S(1)} %bitcast.69), channel_id=1, source_target_pairs={{0,2},{1,3},{2,0},{3,1},{4,6},{5,7},{6,4},{7,5},{8,10},{9,11},{10,... | collective-permute-start | bytes 345608 | tf_op jit(solution)/shard_map/ppermute | solution.py:24
  18.6 6.6 %collective-permute-start.4 = (bf16[450,128]{1,0:T(8,128)(2,1)S(1)}, bf16[450,128]{1,0:T(8,128)(2,1)S(1)}, u32[]{:S(2)}, u32[]{:S(2)}) collective-permute-start(bf16[450,128]{1,0:T(8,128)(2,1)S(1)} %bitcast.68), channel_id=1, source_target_pairs={{0,3},{1,2},{2,1},{3,0},{4,7},{5,6},{6,5},{7,4},{8,11},{9,10},{10,... | collective-permute-start | bytes 345608 | tf_op jit(solution)/shard_map/ppermute | solution.py:24
  19.0 7.0 %collective-permute-start.5 = (bf16[450,128]{1,0:T(8,128)(2,1)S(1)}, bf16[450,128]{1,0:T(8,128)(2,1)S(1)}, u32[]{:S(2)}, u32[]{:S(2)}) collective-permute-start(bf16[450,128]{1,0:T(8,128)(2,1)S(1)} %bitcast.67), channel_id=1, source_target_pairs={{0,4},{1,5},{2,6},{3,7},{4,0},{5,1},{6,2},{7,3},{8,12},{9,13},{10,... | collective-permute-start | bytes 345608 | tf_op jit(solution)/shard_map/ppermute | solution.py:24
  19.2 15.7 %collective-permute-start.6 = (bf16[450,128]{1,0:T(8,128)(2,1)S(1)}, bf16[450,128]{1,0:T(8,128)(2,1)S(1)}, u32[]{:S(2)}, u32[]{:S(2)}) collective-permute-start(bf16[450,128]{1,0:T(8,128)(2,1)S(1)} %bitcast.66), channel_id=1, source_target_pairs={{0,5},{1,4},{2,7},{3,6},{4,1},{5,0},{6,3},{7,2},{8,13},{9,12},{10,... | collective-permute-start | bytes 345608 | tf_op jit(solution)/shard_map/ppermute | solution.py:24
  21.9 18.5 %collective-permute-start.7 = (bf16[450,128]{1,0:T(8,128)(2,1)S(1)}, bf16[450,128]{1,0:T(8,128)(2,1)S(1)}, u32[]{:S(2)}, u32[]{:S(2)}) collective-permute-start(bf16[450,128]{1,0:T(8,128)(2,1)S(1)} %bitcast.65), channel_id=1, source_target_pairs={{0,6},{1,7},{2,4},{3,5},{4,2},{5,3},{6,0},{7,1},{8,14},{9,15},{10,... | collective-permute-start | bytes 345608 | tf_op jit(solution)/shard_map/ppermute | solution.py:24
  22.0 20.9 %collective-permute-start.8 = (bf16[450,128]{1,0:T(8,128)(2,1)S(1)}, bf16[450,128]{1,0:T(8,128)(2,1)S(1)}, u32[]{:S(2)}, u32[]{:S(2)}) collective-permute-start(bf16[450,128]{1,0:T(8,128)(2,1)S(1)} %bitcast.64), channel_id=1, source_target_pairs={{0,7},{1,6},{2,5},{3,4},{4,3},{5,2},{6,1},{7,0},{8,15},{9,14},{10,... | collective-permute-start | bytes 345608 | tf_op jit(solution)/shard_map/ppermute | solution.py:24
